TPU v7x, 32 devices: a whole 2x2x4 slice. The times are simulated.
32 devices in a mesh: sub: 8 (over y, x, core), row: 4 (over z).
Axes of the slice: x: 2, y: 2, z: 4, core: 2. Of those that a mesh axis runs over, the one named last changes fastest.
Arguments:
- basis: bfloat16 [8, 49152, 128], P('sub', 'row'), may hold values from -0.40234375 to 0.40234375
- local_operator: bfloat16 [8, 49152, 384], P('sub', 'row'), may hold values from -0.3125 to 0.3125
- coupling: bfloat16 [3, 8, 4, 2, 128, 128], P(None, 'sub', 'row'), may hold values from -0.5 to 0.5
- partners: int32 [3, 8], replicated, may hold values from 0 to 7, as said below
- margin_blocks: int32 [3, 8, 4, 2], P(None, 'sub', 'row'), may hold values from 0 to 95, as said below
Outputs:
- coarse_tiles: float32 [8, 4, 128, 128], P('sub', None, 'row')
Inputs may be any that keep to these rules, and one draw needn't show every extreme that they name: In every round the partners form a perfect matching: partners[r, partners[r, s]] = s and partners[r, s] != s. `margin_blocks`: for each round, subdomain and device row the 2 entries are different row blocks of that device.
All inputs are finite; a program needn't handle non-finite values.
Results may differ from a plain program's by a relative error of at most 0.0003.
Values may be sent and summed in bfloat16 or wider, within the bound.
A program may use at most 128 MiB of HBM per device.

v0:
```python
import functools

import jax
import jax.numpy as jnp
from jax import lax
from jax.experimental import pallas as pl
from jax.experimental.pallas import tpu as pltpu
from jax.sharding import PartitionSpec as P

MESH = pl.DeviceIdType.MESH
GROUP = 4
TN = (((0,), (0,)), ((), ()))


def split(value):
    high = value.astype(jnp.bfloat16)
    low = (value - high.astype(jnp.float32)).astype(jnp.bfloat16)
    return jnp.concatenate([high, low], axis=1)


def kernel(
    nsub, nrow, partners, margins, basis, operator, coupling, out,
    zpad, gbuf, cbuf, halo, gath, outbox, inbox, acc,
    dsend, osend, drecv, orecv,
    zsem, gsem, csem, hsend, hrecv, psend, precv, bsend, brecv,
    dss, dsr, oss, osr,
):
    sub = lax.axis_index("sub")
    row = lax.axis_index("row")
    chips = nsub // 2
    chip = sub // 2
    core = sub % 2
    mate = chip * 2 + (1 - core)
    count = basis.shape[0]
    groups = count // GROUP
    rounds = margins.shape[0]
    ovl = margins.shape[1]
    share = out.shape[1]
    blk = basis.shape[1]
    width = basis.shape[2]

    def zcopy(g):
        return pltpu.make_async_copy(
            basis.at[pl.ds(g * GROUP, GROUP)], zpad.at[pl.ds(g * GROUP + 1, GROUP)], zsem.at[g]
        )

    def gcopy(g):
        return pltpu.make_async_copy(
            operator.at[pl.ds(g * GROUP, GROUP)], gbuf.at[pl.ds(g * GROUP, GROUP)], gsem.at[g]
        )

    ccopy = pltpu.make_async_copy(coupling, cbuf, csem)

    def each(lower, upper, body):
        lax.fori_loop(lower, upper, lambda i, _: (body(i), 0)[1], 0)

    each(0, groups, lambda g: zcopy(g).start())
    each(0, groups, lambda g: gcopy((g + 1) % groups).start())
    ccopy.start()

    barrier = pltpu.get_barrier_semaphore()
    for step in range(1, chips):
        peer = ((chip + step) % chips) * 2 + core
        pl.semaphore_signal(barrier, inc=1, device_id=(peer, row), device_id_type=MESH)
    pl.semaphore_signal(barrier, inc=1, device_id=(mate, row), device_id_type=MESH)
    for step in range(1, nrow):
        pl.semaphore_signal(
            barrier, inc=1, device_id=(sub, (row + step) % nrow), device_id_type=MESH
        )
    pl.semaphore_wait(barrier, chips + nrow - 1)

    up = pltpu.make_async_remote_copy(
        basis.at[count - 1], halo.at[0], hsend.at[0], hrecv.at[0],
        device_id=(sub, (row + 1) % nrow), device_id_type=MESH,
    )
    down = pltpu.make_async_remote_copy(
        basis.at[0], halo.at[1], hsend.at[1], hrecv.at[1],
        device_id=(sub, (row + nrow - 1) % nrow), device_id_type=MESH,
    )

    @pl.when(row < nrow - 1)
    def _():
        up.start()

    @pl.when(row > 0)
    def _():
        down.start()

    each(0, groups, lambda g: zcopy(g).wait())
    for turn in range(rounds):
        for b in range(ovl):
            gath[chip, turn * ovl + b] = zpad[margins[turn, b] + 1]

    def packet(step):
        return pltpu.make_async_remote_copy(
            gath.at[chip], gath.at[chip], psend.at[step], precv.at[step],
            device_id=(((chip + step) % chips) * 2 + core, row), device_id_type=MESH,
        )

    def arrival(step):
        source = (chip + chips - step) % chips
        return pltpu.make_async_remote_copy(
            gath.at[source], gath.at[source], psend.at[step], precv.at[step],
            device_id=(source * 2 + core, row), device_id_type=MESH,
        )

    for step in range(1, chips):
        packet(step).start()

    acc[...] = jnp.zeros_like(acc)

    def work(g):
        first = g * GROUP
        parts = []
        for j in range(GROUP):
            near = zpad[pl.ds(first + j, 3)].reshape(3 * blk, width)
            image = jnp.dot(gbuf[first + j], near, preferred_element_type=jnp.float32)
            parts.append(split(image))
        own = zpad[pl.ds(first + 1, GROUP)].reshape(GROUP * blk, width)
        acc[...] += lax.dot_general(
            own, jnp.concatenate(parts, axis=0), TN, preferred_element_type=jnp.float32
        )

    def middle(g):
        gcopy(g).wait()
        work(g)

    each(1, groups - 1, middle)

    @pl.when(row > 0)
    def _():
        up.wait_recv()
        zpad[0] = halo[0]

    @pl.when(row == 0)
    def _():
        zpad[0] = jnp.zeros((blk, width), jnp.bfloat16)

    @pl.when(row < nrow - 1)
    def _():
        down.wait_recv()
        zpad[count + 1] = halo[1]

    @pl.when(row == nrow - 1)
    def _():
        zpad[count + 1] = jnp.zeros((blk, width), jnp.bfloat16)

    each(0, 2, lambda i: middle(i * (groups - 1)))

    tile = acc[:, :width] + acc[:, width:]
    dsend[...] = tile.reshape(nrow, share, width)

    def share_out(step, source, target, ss, sr):
        there = (row + step) % nrow
        return pltpu.make_async_remote_copy(
            source.at[there], target.at[step - 1], ss.at[step - 1], sr.at[step - 1],
            device_id=(sub, there), device_id_type=MESH,
        )

    for step in range(1, nrow):
        share_out(step, dsend, drecv, dss, dsr).start()

    for step in range(1, chips):
        arrival(step).wait_recv()
    for turn in range(rounds):
        wanted = partners[turn, mate] // 2
        for b in range(ovl):
            outbox[turn * ovl + b] = gath[wanted, turn * ovl + b]
    cross = pltpu.make_async_remote_copy(
        outbox, inbox, bsend, brecv, device_id=(mate, row), device_id_type=MESH
    )
    cross.start()
    ccopy.wait()
    cross.wait_recv()
    for turn in range(rounds):
        wanted = partners[turn, sub]
        here = jnp.full((blk, width), wanted % 2, jnp.int32) == core
        parts = []
        for b in range(ovl):
            k = turn * ovl + b
            near = gath[wanted // 2, k].astype(jnp.float32)
            far = inbox[k].astype(jnp.float32)
            other = jnp.where(here, near, far).astype(jnp.bfloat16)
            parts.append(split(jnp.dot(cbuf[k], other, preferred_element_type=jnp.float32)))
        own = gath[chip, pl.ds(turn * ovl, ovl)].reshape(ovl * blk, width)
        both = lax.dot_general(
            own, jnp.concatenate(parts, axis=0), TN, preferred_element_type=jnp.float32
        )
        osend[:, turn] = (both[:, :width] + both[:, width:]).reshape(nrow, share, width)
    for step in range(1, nrow):
        share_out(step, osend, orecv, oss, osr).start()

    total = dsend[row]
    for step in range(1, nrow):
        share_out(step, dsend, drecv, dss, dsr).wait_recv()
        total += drecv[step - 1]
    out[0] = total
    total = osend[row]
    for step in range(1, nrow):
        share_out(step, osend, orecv, oss, osr).wait_recv()
        total += orecv[step - 1]
    out[1:] = total

    @pl.when(row < nrow - 1)
    def _():
        up.wait_send()

    @pl.when(row > 0)
    def _():
        down.wait_send()

    for step in range(1, chips):
        packet(step).wait_send()
    cross.wait_send()
    for step in range(1, nrow):
        share_out(step, dsend, drecv, dss, dsr).wait_send()
        share_out(step, osend, orecv, oss, osr).wait_send()


def local(nsub, nrow, basis, local_operator, coupling, partners, margin_blocks):
    rounds, _, _, ovl, blk, _ = coupling.shape
    rows, width = basis.shape[1:]
    count = rows // blk
    groups = count // GROUP
    share = width // nrow
    chips = nsub // 2
    bf16, f32 = jnp.bfloat16, jnp.float32
    dma = pltpu.SemaphoreType.DMA
    any_space = pl.BlockSpec(memory_space=pl.ANY)
    smem = pl.BlockSpec(memory_space=pltpu.SMEM)
    out = pl.pallas_call(
        functools.partial(kernel, nsub, nrow),
        out_shape=jax.ShapeDtypeStruct((1 + rounds, share, width), f32),
        in_specs=[smem, smem, any_space, any_space, any_space],
        out_specs=pl.BlockSpec(memory_space=pltpu.VMEM),
        scratch_shapes=[
            pltpu.VMEM((count + 2, blk, width), bf16),
            pltpu.VMEM((count, blk, 3 * blk), bf16),
            pltpu.VMEM((rounds * ovl, blk, blk), bf16),
            pltpu.VMEM((2, blk, width), bf16),
            pltpu.VMEM((chips, rounds * ovl, blk, width), bf16),
            pltpu.VMEM((rounds * ovl, blk, width), bf16),
            pltpu.VMEM((rounds * ovl, blk, width), bf16),
            pltpu.VMEM((width, 2 * width), f32),
            pltpu.VMEM((nrow, share, width), f32),
            pltpu.VMEM((nrow, rounds, share, width), f32),
            pltpu.VMEM((nrow - 1, share, width), f32),
            pltpu.VMEM((nrow - 1, rounds, share, width), f32),
            dma((groups,)), dma((groups,)), dma(()), dma((2,)), dma((2,)),
            dma((chips,)), dma((chips,)), dma(()), dma(()),
            dma((nrow - 1,)), dma((nrow - 1,)), dma((nrow - 1,)), dma((nrow - 1,)),
        ],
        compiler_params=pltpu.CompilerParams(
            collective_id=0, has_side_effects=True, vmem_limit_bytes=56 << 20
        ),
        name="coarse",
    )(
        partners,
        margin_blocks.reshape(rounds, ovl),
        basis.reshape(count, blk, width),
        local_operator.reshape(count, blk, 3 * blk),
        coupling.reshape(rounds * ovl, blk, blk),
    )
    return out[None]


def solution(mesh):
    placed = (
        P("sub", "row", None),
        P("sub", "row", None),
        P(None, "sub", "row", None, None, None),
        P(),
        P(None, "sub", "row", None),
    )
    body = functools.partial(local, mesh.shape["sub"], mesh.shape["row"])
    return jax.shard_map(
        body, mesh=mesh, in_specs=placed, out_specs=P("sub", None, "row", None), check_vma=False
    )
```

profile of v0, /device:TPU:0, one launch (start us, length us, event | category | flops | bytes accessed | tf_op | source)
XLA Modules:
  0.0 28.5 jit_solution(5430715439645843900)
XLA Ops:
  0.0 1.3 %copy.6.margins = s32[3,2]{1,0:T(4,128)} copy(s32[3,2]{0,1:T(2,128)} %bitcast.9) | data formatting | bytes 48 | tf_op jit(solution)/shard_map/reshape | solution.py:259
  1.3 25.7 %coarse.1 = f32[4,32,128]{2,1,0:T(8,128)} custom-call(s32[3,8]{1,0:T(4,128)} %partners.1, s32[3,2]{1,0:T(4,128)} %copy.6.margins, bf16[96,128,128]{2,1,0:T(8,128)(2,1)} %bitcast.6, bf16[96,128,384]{2,1,0:T(8,128)(2,1)} %bitcast.5, bf16[6,128,128]{2,1,0:T(8,128)(2,1)} %bitcast.8), custom_call_target="tpu_custom_call" | custom-call | tf_op jit(solution)/shard_map/coarse/pallas_call | solution.py:231
  27.0 1.5 %copy.8 = f32[1,4,32,128]{3,2,1,0:T(8,128)} copy(f32[1,4,32,128]{3,2,1,0:T(8,128)} %bitcast.7) | data formatting | bytes 131072
where the time goes:
time: 28.7 us; the launch traced here: 28.5 us
  Pallas kernels  25.7 us (90%)
  local copies, waits for them, and re-layouts  2.81 us (10%)
    pallas_call x1, Pallas kernels, local(): pl.pallas_call(functools.partial(kernel, nsub, nrow), out_shape=jax.Shape...  25.7 us
    unnamed x1, local copies, waits for them, and re-layouts  1.47 us
    reshape x1, local copies, waits for them, and re-layouts, local(): margin_blocks.reshape(rounds, ovl)  1.34 us

commit v1 on v0

v1 whole, which is shorter than its diff:
```python
import functools

import jax
import jax.numpy as jnp
from jax import lax
from jax.experimental import pallas as pl
from jax.experimental.pallas import tpu as pltpu
from jax.sharding import PartitionSpec as P

MESH = pl.DeviceIdType.MESH
GROUP = 8
MARKS = (7, 8, 9, 10, 10)
TN = (((0,), (0,)), ((), ()))


def split(value):
    high = value.astype(jnp.bfloat16)
    low = (value - high.astype(jnp.float32)).astype(jnp.bfloat16)
    return jnp.concatenate([high, low], axis=1)


def kernel(
    nsub, nrow, partners, margins, basis, operator, coupling, out,
    zpad, gbuf, cbuf, halo, gath, outbox, inbox, acc,
    tsend, trecv,
    zsem, gsem, csem, hsend, hrecv, psend, precv, bsend, brecv,
    tss, tsr,
):
    sub = lax.axis_index("sub")
    row = lax.axis_index("row")
    chips = nsub // 2
    chip = sub // 2
    core = sub % 2
    mate = chip * 2 + (1 - core)
    count = basis.shape[0]
    groups = count // GROUP
    rounds = margins.shape[1]
    ovl = margins.shape[0]
    share = out.shape[1]
    blk = basis.shape[1]
    width = basis.shape[2]

    def zcopy(g):
        return pltpu.make_async_copy(
            basis.at[pl.ds(g * GROUP, GROUP)], zpad.at[pl.ds(g * GROUP + 1, GROUP)], zsem.at[g]
        )

    def gcopy(g):
        return pltpu.make_async_copy(
            operator.at[pl.ds(g * GROUP, GROUP)], gbuf.at[pl.ds(g * GROUP, GROUP)], gsem.at[g]
        )

    ccopy = pltpu.make_async_copy(coupling, cbuf, csem)

    def each(lower, upper, body):
        lax.fori_loop(lower, upper, lambda i, _: (body(i), 0)[1], 0)

    barrier = pltpu.get_barrier_semaphore()
    for step in range(1, chips):
        peer = ((chip + step) % chips) * 2 + core
        pl.semaphore_signal(barrier, inc=1, device_id=(peer, row), device_id_type=MESH)
    pl.semaphore_signal(barrier, inc=1, device_id=(mate, row), device_id_type=MESH)
    for step in range(1, nrow):
        pl.semaphore_signal(
            barrier, inc=1, device_id=(sub, (row + step) % nrow), device_id_type=MESH
        )
    each(0, groups, lambda g: zcopy(g).start())
    pl.semaphore_wait(barrier, chips + nrow - 1)

    up = pltpu.make_async_remote_copy(
        basis.at[count - 1], halo.at[0], hsend.at[0], hrecv.at[0],
        device_id=(sub, (row + 1) % nrow), device_id_type=MESH,
    )
    down = pltpu.make_async_remote_copy(
        basis.at[0], halo.at[1], hsend.at[1], hrecv.at[1],
        device_id=(sub, (row + nrow - 1) % nrow), device_id_type=MESH,
    )

    @pl.when(row < nrow - 1)
    def _():
        up.start()

    @pl.when(row > 0)
    def _():
        down.start()

    each(0, groups, lambda g: zcopy(g).wait())
    def packet(turn, step):
        held = gath[turn]
        return pltpu.make_async_remote_copy(
            held.at[chip], held.at[chip], psend.at[turn, step], precv.at[turn, step],
            device_id=(((chip + step) % chips) * 2 + core, row), device_id_type=MESH,
        )

    def arrival(turn, step):
        held = gath[turn]
        source = (chip + chips - step) % chips
        return pltpu.make_async_remote_copy(
            held.at[source], held.at[source], psend.at[turn, step], precv.at[turn, step],
            device_id=(source * 2 + core, row), device_id_type=MESH,
        )

    def cross(turn):
        return pltpu.make_async_remote_copy(
            outbox[turn], inbox[turn], bsend.at[turn], brecv.at[turn],
            device_id=(mate, row), device_id_type=MESH,
        )

    for turn in range(rounds):
        for b in range(ovl):
            gath[turn][chip, b] = zpad[margins[b, turn] + 1]
        for step in range(1, chips):
            packet(turn, step).start()

    each(0, groups, lambda g: gcopy((g + 1) % groups).start())
    ccopy.start()

    acc[...] = jnp.zeros_like(acc)

    def work(g):
        first = g * GROUP
        parts = []
        for j in range(GROUP):
            near = zpad[pl.ds(first + j, 3)].reshape(3 * blk, width)
            image = jnp.dot(gbuf[first + j], near, preferred_element_type=jnp.float32)
            parts.append(split(image))
        own = zpad[pl.ds(first + 1, GROUP)].reshape(GROUP * blk, width)
        acc[...] += lax.dot_general(
            own, jnp.concatenate(parts, axis=0), TN, preferred_element_type=jnp.float32
        )

    def middle(g):
        gcopy(g).wait()
        work(g)

    def share_out(step, turn):
        there = (row + step) % nrow
        return pltpu.make_async_remote_copy(
            tsend.at[turn, there], trecv.at[turn, step - 1],
            tss.at[turn, step - 1], tsr.at[turn, step - 1],
            device_id=(sub, there), device_id_type=MESH,
        )

    def give(turn, both):
        tsend[turn] = (both[:, :width] + both[:, width:]).reshape(nrow, share, width)
        for step in range(1, nrow):
            share_out(step, turn).start()

    def collect(turn):
        total = tsend[turn, row]
        for step in range(1, nrow):
            share_out(step, turn).wait_recv()
            total += trecv[turn, step - 1]
        out[turn] = total

    def hand_over(turn):
        for step in range(1, chips):
            arrival(turn, step).wait_recv()
        wanted = partners[turn, mate] // 2
        for b in range(ovl):
            outbox[turn][b] = gath[turn][wanted, b]
        cross(turn).start()

    def couple(turn):
        wanted = partners[turn, sub]
        here = jnp.full((blk, width), wanted % 2, jnp.int32) == core
        parts = []
        cross(turn).wait_recv()
        for b in range(ovl):
            near = gath[turn][wanted // 2, b].astype(jnp.float32)
            far = inbox[turn][b].astype(jnp.float32)
            other = jnp.where(here, near, far).astype(jnp.bfloat16)
            parts.append(
                split(jnp.dot(cbuf[turn * ovl + b], other, preferred_element_type=jnp.float32))
            )
        own = gath[turn][chip].reshape(ovl * blk, width)
        give(turn + 1, lax.dot_general(
            own, jnp.concatenate(parts, axis=0), TN, preferred_element_type=jnp.float32
        ))

    def edges():
        @pl.when(row > 0)
        def _():
            up.wait_recv()
            zpad[0] = halo[0]

        @pl.when(row == 0)
        def _():
            zpad[0] = jnp.zeros((blk, width), jnp.bfloat16)

        @pl.when(row < nrow - 1)
        def _():
            down.wait_recv()
            zpad[count + 1] = halo[1]

        @pl.when(row == nrow - 1)
        def _():
            zpad[count + 1] = jnp.zeros((blk, width), jnp.bfloat16)

        each(0, 2, lambda i: middle(i * (groups - 1)))

    inner = groups - 2
    marks = [1 + inner * k // 10 for k in MARKS]
    each(1, marks[0], middle)
    ccopy.wait()
    for turn in range(rounds - 1):
        hand_over(turn)
        each(marks[2 * turn], marks[2 * turn + 1], middle)
        couple(turn)
        each(marks[2 * turn + 1], marks[2 * turn + 2], middle)
    each(marks[-1], groups - 1, middle)
    edges()
    give(0, acc[...])
    hand_over(rounds - 1)
    couple(rounds - 1)
    for turn in range(rounds):
        collect(turn)
    collect(rounds)

    @pl.when(row < nrow - 1)
    def _():
        up.wait_send()

    @pl.when(row > 0)
    def _():
        down.wait_send()

    for turn in range(rounds):
        for step in range(1, chips):
            packet(turn, step).wait_send()
        cross(turn).wait_send()
    for turn in range(rounds + 1):
        for step in range(1, nrow):
            share_out(step, turn).wait_send()


def local(nsub, nrow, basis, local_operator, coupling, partners, margin_blocks):
    rounds, _, _, ovl, blk, _ = coupling.shape
    rows, width = basis.shape[1:]
    count = rows // blk
    groups = count // GROUP
    share = width // nrow
    chips = nsub // 2
    bf16, f32 = jnp.bfloat16, jnp.float32
    dma = pltpu.SemaphoreType.DMA
    any_space = pl.BlockSpec(memory_space=pl.ANY)
    smem = pl.BlockSpec(memory_space=pltpu.SMEM)
    out = pl.pallas_call(
        functools.partial(kernel, nsub, nrow),
        out_shape=jax.ShapeDtypeStruct((1 + rounds, share, width), f32),
        in_specs=[smem, smem, any_space, any_space, any_space],
        out_specs=pl.BlockSpec(memory_space=pltpu.VMEM),
        scratch_shapes=[
            pltpu.VMEM((count + 2, blk, width), bf16),
            pltpu.VMEM((count, blk, 3 * blk), bf16),
            pltpu.VMEM((rounds * ovl, blk, blk), bf16),
            pltpu.VMEM((2, blk, width), bf16),
            [pltpu.VMEM((chips, ovl, blk, width), bf16) for _ in range(rounds)],
            [pltpu.VMEM((ovl, blk, width), bf16) for _ in range(rounds)],
            [pltpu.VMEM((ovl, blk, width), bf16) for _ in range(rounds)],
            pltpu.VMEM((width, 2 * width), f32),
            pltpu.VMEM((1 + rounds, nrow, share, width), f32),
            pltpu.VMEM((1 + rounds, nrow - 1, share, width), f32),
            dma((groups,)), dma((groups,)), dma(()), dma((2,)), dma((2,)),
            dma((rounds, chips)), dma((rounds, chips)), dma((rounds,)), dma((rounds,)),
            dma((1 + rounds, nrow - 1)), dma((1 + rounds, nrow - 1)),
        ],
        compiler_params=pltpu.CompilerParams(
            collective_id=0, has_side_effects=True, vmem_limit_bytes=56 << 20
        ),
        name="coarse",
    )(
        partners,
        margin_blocks[:, 0, 0].T,
        basis.reshape(count, blk, width),
        local_operator.reshape(count, blk, 3 * blk),
        coupling.reshape(rounds * ovl, blk, blk),
    )
    return out[None]


def solution(mesh):
    placed = (
        P("sub", "row", None),
        P("sub", "row", None),
        P(None, "sub", "row", None, None, None),
        P(),
        P(None, "sub", "row", None),
    )
    body = functools.partial(local, mesh.shape["sub"], mesh.shape["row"])
    return jax.shard_map(
        body, mesh=mesh, in_specs=placed, out_specs=P("sub", None, "row", None), check_vma=False
    )
```

time: 28.7 us -> 25.6 us (0.89)
  Pallas kernels: 25.7 us -> 23.9 us
  local copies, waits for them, and re-layouts: 2.81 us -> 1.47 us
    pallas_call x1, Pallas kernels: 25.7 us -> 23.9 us  [local(): pl.pallas_call(functools.partial(kernel, nsub, nrow), out_shape=jax.Shape...]
    reshape x1 -> x0, local copies, waits for them, and re-layouts: 1.34 us -> none  [local(): margin_blocks.reshape(rounds, ovl)]
where the time goes in v1:
time: 25.6 us; the launch traced here: 25.4 us
  Pallas kernels  23.9 us (93%)
  local copies, waits for them, and re-layouts  1.47 us (6%)
    pallas_call x1, Pallas kernels, local(): pl.pallas_call(functools.partial(kernel, nsub, nrow), out_shape=jax.Shape...  23.9 us
    unnamed x1, local copies, waits for them, and re-layouts  1.47 us

profile of v1, /device:TPU:0, one launch (start us, length us, event | category | flops | bytes accessed | tf_op | source)
XLA Modules:
  0.0 25.4 jit_solution(7126951676099814751)
XLA Ops:
  0.0 23.9 %coarse.1 = f32[4,32,128]{2,1,0:T(8,128)} custom-call(s32[3,8]{1,0:T(4,128)} %partners.1, s32[2,3]{1,0:T(2,128)} %bitcast.11, bf16[96,128,128]{2,1,0:T(8,128)(2,1)} %bitcast.8, bf16[96,128,384]{2,1,0:T(8,128)(2,1)} %bitcast.7, bf16[6,128,128]{2,1,0:T(8,128)(2,1)} %bitcast.10), custom_call_target="tpu_custom_call" | custom-call | tf_op jit(solution)/shard_map/coarse/pallas_call | solution.py:248
  23.9 1.5 %copy.7 = f32[1,4,32,128]{3,2,1,0:T(8,128)} copy(f32[1,4,32,128]{3,2,1,0:T(8,128)} %bitcast.9) | data formatting | bytes 131072

commit v2 on v1

--- a/solution.py
+++ b/solution.py
@@ -208,10 +208,10 @@
         each(marks[2 * turn], marks[2 * turn + 1], middle)
         couple(turn)
         each(marks[2 * turn + 1], marks[2 * turn + 2], middle)
+    hand_over(rounds - 1)
     each(marks[-1], groups - 1, middle)
     edges()
     give(0, acc[...])
-    hand_over(rounds - 1)
     couple(rounds - 1)
     for turn in range(rounds):
         collect(turn)

time: 25.6 us -> 25.7 us (level)
  no operation moved by 1% of the time
where the time goes in v2:
time: 25.7 us; the launch traced here: 25.5 us
  Pallas kernels  24 us (93%)
  local copies, waits for them, and re-layouts  1.47 us (6%)
    pallas_call x1, Pallas kernels, local(): pl.pallas_call(functools.partial(kernel, nsub, nrow), out_shape=jax.Shape...  24 us
    unnamed x1, local copies, waits for them, and re-layouts  1.47 us

profile of v2, /device:TPU:0, one launch (start us, length us, event | category | flops | bytes accessed | tf_op | source)
XLA Modules:
  0.0 25.5 jit_solution(10929514406276654198)
XLA Ops:
  0.0 24.0 %coarse.1 = f32[4,32,128]{2,1,0:T(8,128)} custom-call(s32[3,8]{1,0:T(4,128)} %partners.1, s32[2,3]{1,0:T(2,128)} %bitcast.11, bf16[96,128,128]{2,1,0:T(8,128)(2,1)} %bitcast.8, bf16[96,128,384]{2,1,0:T(8,128)(2,1)} %bitcast.7, bf16[6,128,128]{2,1,0:T(8,128)(2,1)} %bitcast.10), custom_call_target="tpu_custom_call" | custom-call | tf_op jit(solution)/shard_map/coarse/pallas_call | solution.py:248
  24.0 1.5 %copy.7 = f32[1,4,32,128]{3,2,1,0:T(8,128)} copy(f32[1,4,32,128]{3,2,1,0:T(8,128)} %bitcast.9) | data formatting | bytes 131072
